TPU v7x, 128 devices: a whole 4x4x4 slice. The times are simulated.
128 devices in a mesh: row: 16 (over z, x_hi, core), col: 8 (over y, x_lo).
Axes of the slice: x: 4 (x_hi: 2, x_lo: 2; x = x_hi * 2 + x_lo), y: 4, z: 4, core: 2. Of those that a mesh axis runs over, the one named last changes fastest.
Arguments:
- queries: bfloat16 [1024, 8192], P('col', 'row'), may hold values from -8 to 8
- cache_keys: bfloat16 [8, 131072, 128], P(None, ('row', 'col')), may hold values from -8 to 8
- cache_values: bfloat16 [8, 131072, 128], P(None, ('row', 'col')), may hold values from -6 to 6
- stretch_keys: bfloat16 [8, 1024, 128], P(None, 'col'), may hold values from -8 to 8
- stretch_values: bfloat16 [8, 1024, 128], P(None, 'col'), may hold values from -6 to 6
- block_lists: int32 [8, 8, 64], replicated, may hold values from 0 to 1023, as said below
- out_weight: bfloat16 [8192, 8192], P('row', 'col'), may hold values from -0.5 to 0.5
- residual: bfloat16 [1024, 8192], P('row', 'col'), may hold values from -6 to 6
- norm_gain: bfloat16 [8192], P('col'), may hold values from 0.25 to 1.75
- gate_weight: bfloat16 [8192, 28672], P('col', 'row'), may hold values from -0.0625 to 0.0625
- up_weight: bfloat16 [8192, 28672], P('col', 'row'), may hold values from -0.0625 to 0.0625
- down_weight: bfloat16 [28672, 8192], P('row', 'col'), may hold values from -0.03125 to 0.03125
Outputs:
- layer_out: bfloat16 [1024, 8192], P('row', 'col')
Inputs may be any that keep to these rules, and one draw needn't show every extreme that they name: `block_lists`: each list names 64 different cache blocks; device k of row+col holds cache blocks k * (8) to (k + 1) * 8 - 1, and no two blocks of one list lie on the same device. Every list holds block 0 and block 1023.
All inputs are finite; a program needn't handle non-finite values.
Results may differ from a plain program's by a relative error of at most 0.0085.
Values may be sent and summed in bfloat16 or wider, within the bound.
No kernel may reach another device: no remote copies, remote signals or barrier semaphores. Data moves between devices by JAX's collectives and lax.ppermute only.
A program may use at most 128 MiB of HBM per device.

v0:
```python
import math
import jax
import jax.numpy as jnp
from jax import lax
from jax.sharding import PartitionSpec as P

D = 8192
KV_HEADS = 8
HEAD_DIM = 128
BLK = 128
GROUP = 8


def local(
    queries,
    cache_keys,
    cache_values,
    stretch_keys,
    stretch_values,
    block_lists,
    out_weight,
    residual,
    norm_gain,
    gate_weight,
    up_weight,
    down_weight,
):
    row_count = lax.axis_size("row")
    col_count = lax.axis_size("col")
    row_index = lax.axis_index("row")
    col_index = lax.axis_index("col")
    device_count = row_count * col_count
    my_index = row_index * col_count + col_index
    local_blocks = cache_keys.shape[1] // BLK
    heads_here = queries.shape[1] // HEAD_DIM
    list_length = block_lists.shape[2]
    my_group = row_index * heads_here // GROUP
    scaling = 1.0 / math.sqrt(HEAD_DIM)
    targets = jnp.arange(device_count, dtype=jnp.int32)
    target_group = targets // col_count * heads_here // GROUP
    target_lists = block_lists[targets % col_count, target_group]
    holders = target_lists // local_blocks
    matched = holders == my_index
    found_any = jnp.any(matched, axis=1)
    within = jnp.sum(jnp.where(matched, target_lists % local_blocks, 0), axis=1)
    source_rows = target_group * local_blocks + within
    flat_keys = cache_keys.reshape(KV_HEADS * local_blocks, BLK, HEAD_DIM)
    flat_values = cache_values.reshape(KV_HEADS * local_blocks, BLK, HEAD_DIM)
    outgoing = jnp.concatenate([flat_keys[source_rows], flat_values[source_rows]], axis=2)
    outgoing = jnp.where(found_any[:, None, None], outgoing, jnp.zeros_like(outgoing))
    arrived = lax.all_to_all(outgoing, ("row", "col"), split_axis=0, concat_axis=0, tiled=True)
    my_list = block_lists[col_index, my_group]
    fetched = arrived[my_list // local_blocks].reshape(list_length * BLK, 2 * HEAD_DIM)
    far_keys = fetched[:, :HEAD_DIM]
    far_values = fetched[:, HEAD_DIM:]
    query_rows = queries.reshape(BLK * heads_here, HEAD_DIM)
    far_scores = jnp.dot(query_rows, far_keys.T, preferred_element_type=jnp.float32) * scaling
    run_max = jnp.max(far_scores, axis=1)
    far_exp = jnp.exp(far_scores - run_max[:, None])
    run_sum = jnp.sum(far_exp, axis=1)
    run_acc = jnp.dot(far_exp.astype(jnp.bfloat16), far_values, preferred_element_type=jnp.float32)
    query_pos = col_index * BLK + jnp.arange(BLK * heads_here, dtype=jnp.int32) // heads_here
    own_keys = lax.dynamic_index_in_dim(stretch_keys, my_group, 0, keepdims=False)
    own_values = lax.dynamic_index_in_dim(stretch_values, my_group, 0, keepdims=False)
    piece_keys = lax.all_gather(own_keys, "col", axis=0, tiled=True)
    piece_values = lax.all_gather(own_values, "col", axis=0, tiled=True)
    scores = jnp.dot(query_rows, piece_keys.T, preferred_element_type=jnp.float32) * scaling
    key_pos = jnp.arange(piece_keys.shape[0], dtype=jnp.int32)
    allowed = key_pos[None, :] <= query_pos[:, None]
    scores = jnp.where(allowed, scores, -1e30)
    new_max = jnp.maximum(run_max, jnp.max(scores, axis=1))
    decays = jnp.exp(run_max - new_max)
    weights = jnp.where(allowed, jnp.exp(scores - new_max[:, None]), 0.0)
    new_sum = run_sum * decays + jnp.sum(weights, axis=1)
    new_acc = run_acc * decays[:, None] + jnp.dot(
        weights.astype(jnp.bfloat16), piece_values, preferred_element_type=jnp.float32
    )
    attended = (new_acc / new_sum[:, None]).astype(jnp.bfloat16).reshape(BLK, heads_here * HEAD_DIM)
    all_attended = lax.all_gather(attended, "col", axis=0, tiled=True)
    projected = lax.psum_scatter(
        jnp.dot(all_attended, out_weight, preferred_element_type=jnp.float32),
        "row",
        scatter_dimension=0,
        tiled=True,
    )
    stream = residual.astype(jnp.float32) + projected
    squares = lax.psum(jnp.sum(stream * stream, axis=1), "col")
    normed = (
        stream * lax.rsqrt(squares / D + 1e-05)[:, None] * norm_gain.astype(jnp.float32)
    ).astype(jnp.bfloat16)
    block_piece = lax.all_gather(normed, "row", axis=0, tiled=True)
    gate_part = jnp.dot(block_piece, gate_weight, preferred_element_type=jnp.float32)
    up_part = jnp.dot(block_piece, up_weight, preferred_element_type=jnp.float32)
    partials = jnp.concatenate([gate_part, up_part], axis=1)
    hidden_width = gate_weight.shape[1]
    summed = lax.psum(partials, "col")
    hidden = (jax.nn.silu(summed[:, :hidden_width]) * summed[:, hidden_width:]).astype(jnp.bfloat16)
    down_terms = jnp.dot(hidden, down_weight, preferred_element_type=jnp.float32)
    mlp_part = lax.psum_scatter(down_terms, "row", scatter_dimension=0, tiled=True)
    return (stream + mlp_part).astype(jnp.bfloat16)


def solution(mesh):
    in_specs = (
        P("col", "row"),
        P(None, ("row", "col"), None),
        P(None, ("row", "col"), None),
        P(None, "col", None),
        P(None, "col", None),
        P(),
        P("row", "col"),
        P("row", "col"),
        P("col"),
        P("col", "row"),
        P("col", "row"),
        P("row", "col"),
    )
    out_specs = P("row", "col")
    return jax.shard_map(local, mesh=mesh, in_specs=in_specs, out_specs=out_specs, check_vma=False)
```

profile of v0, /device:TPU:0, one launch (start us, length us, event | category | flops | bytes accessed | tf_op | source)
XLA Modules:
  0.0 1105.7 jit_solution(4571468520694999564)
XLA Ops:
  6.6 1.9 gather_fusion
  8.4 0.1 fusion.48
  8.6 0.1 fusion.26
  8.7 0.0 copy-done
  8.7 3.1 gather_fusion.2
  11.8 4.6 gather_fusion.1
  16.4 8.2 maximum_select_fusion
  24.6 11.7 %all-to-all-start = ((bf16[128,128,256]{2,1,0:T(8,128)(2,1)}), bf16[128,128,256]{2,1,0:T(8,128)(2,1)}, u32[]{:S(2)}, u32[]{:S(2)}) async-start(bf16[128,128,256]{2,1,0:T(8,128)(2,1)} %maximum_select_fusion), calls=%async_computation | async-start | bytes 16777216 | tf_op jit(solution)/shard_map/all_to_all | solution.py:51
  36.3 0.0 all-gather.5.cloned.1.call-start
  36.4 0.1 reshape.272
  36.5 0.7 fusion.41
  37.2 0.8 constant_dynamic-slice_fusion.1
  38.0 0.8 constant_dynamic-slice_fusion
  38.7 118.4 %all-gather.1 = bf16[1,1024,128]{2,1,0:T(8,128)(2,1)S(1)} all-gather(bf16[1,128,128]{2,1,0:T(8,128)(2,1)S(1)} %constant_dynamic-slice_fusion), channel_id=3, replica_groups=mesh['row'=16,'col'=8] {'col'}, dimensions={1}, use_global_device_ids=true | all-gather | bytes 294912 | tf_op jit(solution)/shard_map/all_gather | solution.py:66
  157.1 28.9 %all-gather = bf16[1,1024,128]{2,1,0:T(8,128)(2,1)S(1)} all-gather(bf16[1,128,128]{2,1,0:T(8,128)(2,1)S(1)} %constant_dynamic-slice_fusion.1), channel_id=2, replica_groups=mesh['row'=16,'col'=8] {'col'}, dimensions={1}, use_global_device_ids=true | all-gather | bytes 294912 | tf_op jit(solution)/shard_map/all_gather | solution.py:65
  186.0 0.5 fusion.10
  186.4 0.0 all-to-all-done
  186.5 6.1 gather_fusion.3
  192.6 9.6 multiply_reduce_fusion
  202.2 8.8 fusion
  211.0 0.6 fusion.11
  211.6 7.7 fusion.15
  219.3 0.8 fusion.14
  220.1 0.7 reshape.273
  220.8 0.0 all-gather.5.cloned.1.call-update
  220.9 0.0 reduce-scatter.3.cloned.1.call-start
  220.9 39.3 %all-gather.5.cloned.1.call-done = bf16[1024,512]{1,0:T(8,128)(2,1)} async-done(((bf16[128,512]{1,0:T(8,128)(2,1)}), bf16[1024,512]{1,0:T(8,128)(2,1)}) %all-gather.5.cloned.1.call-update) | async-done | bytes 1048592 | tf_op jit(solution)/shard_map/all_gather | solution.py:79
  260.3 4.7 fusion.50
  265.0 0.0 reduce-scatter.3.cloned.1.call-update
  265.0 0.0 all-gather.7.cloned.1.call-start
  265.1 0.6 copy-done.6
  265.7 79.7 %reduce-scatter.3.cloned.1.call-done = f32[64,1024]{1,0:T(8,128)} async-done(((f32[1024,1024]{1,0:T(8,128)}), f32[64,1024]{1,0:T(8,128)}) %reduce-scatter.3.cloned.1.call-update) | async-done | bytes 262160 | tf_op jit(solution)/shard_map/reduce_scatter | solution.py:80
  345.4 1.1 multiply_reduce_fusion.1
  346.4 18.8 %psum.14 = f32[64]{0:T(128)S(1)} all-reduce(f32[64]{0:T(128)S(1)} %multiply_reduce_fusion.1), channel_id=1, replica_groups=mesh['row'=16,'col'=8] {'col'}, use_global_device_ids=true, to_apply=%region_8.9 | all-reduce | flops 64 | bytes 512 | tf_op jit(solution)/shard_map/psum | solution.py:87
  365.2 1.7 multiply_convert_fusion
  366.9 0.0 all-gather.7.cloned.1.call-update
  367.0 0.3 all-reduce.2.cloned.1.call-start
  367.2 44.7 %all-gather.7.cloned.1.call-done = bf16[1024,1024]{1,0:T(8,128)(2,1)} async-done(((bf16[64,1024]{1,0:T(8,128)(2,1)}), bf16[1024,1024]{1,0:T(8,128)(2,1)}) %all-gather.7.cloned.1.call-update) | async-done | bytes 2097168 | tf_op jit(solution)/shard_map/all_gather | solution.py:91
  412.0 6.8 fusion.52
  418.8 4.0 fusion.51
  422.7 5.7 pad_maximum_fusion
  428.5 0.0 all-reduce.2.cloned.1.call-update
  428.5 0.0 reduce-scatter.5.cloned.1.call-start
  428.5 574.8 %all-reduce.2.cloned.1.call-done = f32[1024,3584]{1,0:T(8,128)} async-done(((f32[1024,3584]{1,0:T(8,128)}), f32[1024,3584]{1,0:T(8,128)}) %all-reduce.2.cloned.1.call-update) | async-done | bytes 14680080 | tf_op jit(solution)/shard_map/psum | solution.py:96
  1003.3 12.3 %fusion.5 = f32[1024,1024]{1,0:T(8,128)} fusion(bf16[1792,1024]{1,0:T(8,128)(2,1)} %param.23, f32[1024,3584]{1,0:T(8,128)} %all-reduce.2.cloned.1.call-done), kind=kOutput, calls=%fused_computation.13 | convolution fusion | flops 3769106432 | bytes 22544384 | tf_op jit(solution)/shard_map/dot_general | solution.py:98
  1015.7 0.0 reduce-scatter.5.cloned.1.call-update
  1015.7 81.9 %reduce-scatter.5.cloned.1.call-done = f32[64,1024]{1,0:T(8,128)} async-done(((f32[1024,1024]{1,0:T(8,128)}), f32[64,1024]{1,0:T(8,128)}) %reduce-scatter.5.cloned.1.call-update) | async-done | bytes 262160 | tf_op jit(solution)/shard_map/reduce_scatter | solution.py:99
  1097.5 1.6 add_convert_fusion
  (25 shorter events, 0.1 us)
Async XLA Ops:
  6.5 2.2 copy-start
  24.6 11.8 %copy-start.5 = (bf16[128,512]{1,0:T(8,128)(2,1)S(1)}, bf16[128,512]{1,0:T(8,128)(2,1)}, u32[]{:S(2)}) copy-start(bf16[128,512]{1,0:T(8,128)(2,1)} %param.12) | copy-start | bytes 393220
  24.6 161.9 %all-to-all-start = ((bf16[128,128,256]{2,1,0:T(8,128)(2,1)}), bf16[128,128,256]{2,1,0:T(8,128)(2,1)}, u32[]{:S(2)}, u32[]{:S(2)}) async-start(bf16[128,128,256]{2,1,0:T(8,128)(2,1)} %maximum_select_fusion), calls=%async_computation | async-start | bytes 16777216 | tf_op jit(solution)/shard_map/all_to_all | solution.py:51
  36.3 224.0 %all-gather.5.cloned.1.call-start = ((), (), s32[]{:S(2)}) async-start(), calls=%async_computation.3 | async-start | bytes 1179648 | tf_op jit(solution)/shard_map/all_gather | solution.py:79
  202.2 9.4 copy-start.2
  220.9 124.5 %reduce-scatter.3.cloned.1.call-start = ((), (), s32[]{:S(2)}) async-start(), calls=%async_computation.4 | async-start | bytes 4456448 | tf_op jit(solution)/shard_map/reduce_scatter | solution.py:80
  265.0 0.7 copy-start.6
  265.0 80.4 %copy-start.4 = (bf16[64,1024]{1,0:T(8,128)(2,1)S(1)}, bf16[64,1024]{1,0:T(8,128)(2,1)}, u32[]{:S(2)}) copy-start(bf16[64,1024]{1,0:T(8,128)(2,1)} %param.19) | copy-start | bytes 393220
  265.0 147.0 %all-gather.7.cloned.1.call-start = ((), (), s32[]{:S(2)}) async-start(), calls=%async_computation.5 | async-start | bytes 2228224 | tf_op jit(solution)/shard_map/all_gather | solution.py:91
  367.0 636.4 %all-reduce.2.cloned.1.call-start = ((), (), s32[]{:S(2)}) async-start(), calls=%async_computation.6 | async-start | bytes 29360128 | tf_op jit(solution)/shard_map/psum | solution.py:96
  412.0 6.8 copy-start.7
  412.0 6.8 copy-start.8
  428.5 669.0 %reduce-scatter.5.cloned.1.call-start = ((), (), s32[]{:S(2)}) async-start(), calls=%async_computation.7 | async-start | bytes 4456448 | tf_op jit(solution)/shard_map/reduce_scatter | solution.py:99
  1003.3 95.9 %copy-start.1 = (bf16[8,1024,128]{2,1,0:T(8,128)(2,1)S(1)}, bf16[8,1024,128]{2,1,0:T(8,128)(2,1)}, u32[]{:S(2)}) copy-start(bf16[8,1024,128]{2,1,0:T(8,128)(2,1)} %param.14) | copy-start | bytes 6291460
  1015.6 81.9 %copy-start.3 = (f32[64,1024]{1,0:T(8,128)S(1)}, f32[64,1024]{1,0:T(8,128)}, u32[]{:S(2)}) copy-start(f32[64,1024]{1,0:T(8,128)} %reduce-scatter.3.cloned.1.call-done) | copy-start | bytes 786436
Sparse Core Ops, SparseCore 0:
  221.0 39.2 all-gather.4
  265.1 80.1 reduce-scatter.2
  367.1 44.8 all-gather.6
  428.6 574.6 all-reduce.1
  1015.8 81.6 reduce-scatter.4
where the time goes:
time: 1110 us
  waiting for transfers between devices  820 us (74%)
  blocking collectives  166 us (15%)
  matrix products  46.4 us (4%)
  other arithmetic  28.8 us (3%)
  local copies, waits for them, and re-layouts  18.7 us (2%)
  between operations  13.3 us (1%)
  starting transfers between devices  12.1 us (1%)
    psum x1, waiting for transfers between devices, local(): summed = lax.psum(partials, 'col')  575 us
    all_gather x1, blocking collectives, local(): piece_values = lax.all_gather(own_values, 'col', axis=0, tiled=True)  118 us
    reduce_scatter x1, waiting for transfers between devices, local(): lax.psum_scatter(down_terms, 'row', scatter_dimension=0, tiled=True)  81.9 us
    reduce_scatter x1, waiting for transfers between devices, local(): lax.psum_scatter(jnp.dot(all_attended, out_weight, preferred_element_type...  79.7 us
    all_gather x1, waiting for transfers between devices, local(): block_piece = lax.all_gather(normed, 'row', axis=0, tiled=True)  44.7 us
    all_gather x1, waiting for transfers between devices, local(): all_attended = lax.all_gather(attended, 'col', axis=0, tiled=True)  39.3 us
    all_gather x1, blocking collectives, local(): piece_keys = lax.all_gather(own_keys, 'col', axis=0, tiled=True)  28.9 us
  transfers between devices with their start and end apart: 6, of which 5 were waited for; matrix products, arithmetic and copies ran while one was open for 0% of the time, Pallas kernels for 0%

commit v1 on v0

--- a/solution.py
+++ b/solution.py
@@ -62,8 +62,11 @@
     query_pos = col_index * BLK + jnp.arange(BLK * heads_here, dtype=jnp.int32) // heads_here
     own_keys = lax.dynamic_index_in_dim(stretch_keys, my_group, 0, keepdims=False)
     own_values = lax.dynamic_index_in_dim(stretch_values, my_group, 0, keepdims=False)
-    piece_keys = lax.all_gather(own_keys, "col", axis=0, tiled=True)
-    piece_values = lax.all_gather(own_values, "col", axis=0, tiled=True)
+    piece_keys, piece_values = jnp.split(
+        lax.all_gather(jnp.concatenate([own_keys, own_values], axis=1), "col", axis=0, tiled=True),
+        [own_keys.shape[1]],
+        axis=1,
+    )
     scores = jnp.dot(query_rows, piece_keys.T, preferred_element_type=jnp.float32) * scaling
     key_pos = jnp.arange(piece_keys.shape[0], dtype=jnp.int32)
     allowed = key_pos[None, :] <= query_pos[:, None]

time: 1110 us -> 1080 us (0.973)
  blocking collectives: 166 us -> 139 us
    all_gather x2 -> x1, blocking collectives: 147 us -> 120 us  [local(): lax.all_gather(jnp.concatenate([own_keys, own_values], axis=1), 'col', ax...]
where the time goes in v1:
time: 1080 us
  waiting for transfers between devices  821 us (76%)
  blocking collectives  139 us (13%)
  matrix products  46.4 us (4%)
  other arithmetic  28.8 us (3%)
  local copies, waits for them, and re-layouts  18.7 us (2%)
  between operations  13.3 us (1%)
  starting transfers between devices  12.1 us (1%)
    psum x1, waiting for transfers between devices, local(): summed = lax.psum(partials, 'col')  575 us
    all_gather x1, blocking collectives, local(): lax.all_gather(jnp.concatenate([own_keys, own_values], axis=1), 'col', ax...  120 us
    reduce_scatter x1, waiting for transfers between devices, local(): lax.psum_scatter(down_terms, 'row', scatter_dimension=0, tiled=True)  81.9 us
    reduce_scatter x1, waiting for transfers between devices, local(): lax.psum_scatter(jnp.dot(all_attended, out_weight, preferred_element_type...  79.7 us
    all_gather x1, waiting for transfers between devices, local(): block_piece = lax.all_gather(normed, 'row', axis=0, tiled=True)  44.7 us
    all_gather x1, waiting for transfers between devices, local(): all_attended = lax.all_gather(attended, 'col', axis=0, tiled=True)  39.5 us
  transfers between devices with their start and end apart: 6, of which 5 were waited for; matrix products, arithmetic and copies ran while one was open for 0% of the time, Pallas kernels for 0%

profile of v1, /device:TPU:0, one launch (start us, length us, event | category | flops | bytes accessed | tf_op | source)
XLA Modules:
  0.0 1078.8 jit_solution(8922365992001146458)
XLA Ops:
  6.6 1.9 gather_fusion
  8.4 0.1 fusion.48
  8.6 0.1 fusion.26
  8.7 0.0 copy-done
  8.7 3.1 gather_fusion.2
  11.8 4.6 gather_fusion.1
  16.4 8.2 maximum_select_fusion
  24.6 11.7 %all-to-all-start = ((bf16[128,128,256]{2,1,0:T(8,128)(2,1)}), bf16[128,128,256]{2,1,0:T(8,128)(2,1)}, u32[]{:S(2)}, u32[]{:S(2)}) async-start(bf16[128,128,256]{2,1,0:T(8,128)(2,1)} %maximum_select_fusion), calls=%async_computation | async-start | bytes 16777216 | tf_op jit(solution)/shard_map/all_to_all | solution.py:51
  36.3 0.0 all-gather.3.cloned.1.call-start
  36.3 0.1 reshape.272
  36.4 0.7 fusion.41
  37.2 0.8 dynamic-slice_bitcast_fusion
  38.0 120.0 %all_gather.9 = bf16[1024,256]{1,0:T(8,128)(2,1)S(1)} all-gather(bf16[128,256]{1,0:T(8,128)(2,1)S(1)} %pad_maximum_fusion.1), channel_id=1, replica_groups=mesh['row'=16,'col'=8] {'col'}, dimensions={0}, use_global_device_ids=true | all-gather | bytes 589824 | tf_op jit(solution)/shard_map/all_gather | solution.py:66
  158.0 0.8 copy-done.5
  158.8 0.5 fusion.10
  159.3 0.0 all-to-all-done
  159.3 6.1 gather_fusion.3
  165.4 9.6 multiply_reduce_fusion
  175.1 8.8 fusion
  183.8 0.6 fusion.11
  184.5 0.0 copy-start.6
  184.5 7.8 fusion.15
  192.3 0.8 fusion.14
  193.0 0.7 reshape.273
  193.8 0.0 all-gather.3.cloned.1.call-update
  193.8 0.0 reduce-scatter.3.cloned.1.call-start
  193.9 39.5 %all-gather.3.cloned.1.call-done = bf16[1024,512]{1,0:T(8,128)(2,1)} async-done(((bf16[128,512]{1,0:T(8,128)(2,1)}), bf16[1024,512]{1,0:T(8,128)(2,1)}) %all-gather.3.cloned.1.call-update) | async-done | bytes 1048592 | tf_op jit(solution)/shard_map/all_gather | solution.py:82
  233.3 4.7 fusion.50
  238.1 0.0 reduce-scatter.3.cloned.1.call-update
  238.1 0.0 all-gather.5.cloned.1.call-start
  238.2 0.6 copy-done.8
  238.8 79.7 %reduce-scatter.3.cloned.1.call-done = f32[64,1024]{1,0:T(8,128)} async-done(((f32[1024,1024]{1,0:T(8,128)}), f32[64,1024]{1,0:T(8,128)}) %reduce-scatter.3.cloned.1.call-update) | async-done | bytes 262160 | tf_op jit(solution)/shard_map/reduce_scatter | solution.py:83
  318.5 1.1 multiply_reduce_fusion.1
  319.5 18.8 %psum.14 = f32[64]{0:T(128)S(1)} all-reduce(f32[64]{0:T(128)S(1)} %multiply_reduce_fusion.1), channel_id=1, replica_groups=mesh['row'=16,'col'=8] {'col'}, use_global_device_ids=true, to_apply=%region_8.9 | all-reduce | flops 64 | bytes 512 | tf_op jit(solution)/shard_map/psum | solution.py:90
  338.3 1.7 multiply_convert_fusion
  340.0 0.0 all-gather.5.cloned.1.call-update
  340.1 0.3 all-reduce.2.cloned.1.call-start
  340.3 44.7 %all-gather.5.cloned.1.call-done = bf16[1024,1024]{1,0:T(8,128)(2,1)} async-done(((bf16[64,1024]{1,0:T(8,128)(2,1)}), bf16[1024,1024]{1,0:T(8,128)(2,1)}) %all-gather.5.cloned.1.call-update) | async-done | bytes 2097168 | tf_op jit(solution)/shard_map/all_gather | solution.py:94
  385.1 6.8 fusion.52
  391.9 4.0 fusion.51
  395.8 5.8 pad_maximum_fusion
  401.6 0.0 all-reduce.2.cloned.1.call-update
  401.6 0.0 reduce-scatter.5.cloned.1.call-start
  401.6 574.8 %all-reduce.2.cloned.1.call-done = f32[1024,3584]{1,0:T(8,128)} async-done(((f32[1024,3584]{1,0:T(8,128)}), f32[1024,3584]{1,0:T(8,128)}) %all-reduce.2.cloned.1.call-update) | async-done | bytes 14680080 | tf_op jit(solution)/shard_map/psum | solution.py:99
  976.4 12.3 %fusion.5 = f32[1024,1024]{1,0:T(8,128)} fusion(bf16[1792,1024]{1,0:T(8,128)(2,1)} %param.23, f32[1024,3584]{1,0:T(8,128)} %all-reduce.2.cloned.1.call-done), kind=kOutput, calls=%fused_computation.13 | convolution fusion | flops 3769106432 | bytes 22544384 | tf_op jit(solution)/shard_map/dot_general | solution.py:101
  988.8 0.0 reduce-scatter.5.cloned.1.call-update
  988.8 81.9 %reduce-scatter.5.cloned.1.call-done = f32[64,1024]{1,0:T(8,128)} async-done(((f32[1024,1024]{1,0:T(8,128)}), f32[64,1024]{1,0:T(8,128)}) %reduce-scatter.5.cloned.1.call-update) | async-done | bytes 262160 | tf_op jit(solution)/shard_map/reduce_scatter | solution.py:102
  1070.6 1.6 add_convert_fusion
  (28 shorter events, 0.1 us)
Async XLA Ops:
  6.5 2.2 copy-start
  24.6 11.8 %copy-start.7 = (bf16[128,512]{1,0:T(8,128)(2,1)S(1)}, bf16[128,512]{1,0:T(8,128)(2,1)}, u32[]{:S(2)}) copy-start(bf16[128,512]{1,0:T(8,128)(2,1)} %param.12) | copy-start | bytes 393220
  24.6 134.7 %all-to-all-start = ((bf16[128,128,256]{2,1,0:T(8,128)(2,1)}), bf16[128,128,256]{2,1,0:T(8,128)(2,1)}, u32[]{:S(2)}, u32[]{:S(2)}) async-start(bf16[128,128,256]{2,1,0:T(8,128)(2,1)} %maximum_select_fusion), calls=%async_computation | async-start | bytes 16777216 | tf_op jit(solution)/shard_map/all_to_all | solution.py:51
  36.3 197.1 %all-gather.3.cloned.1.call-start = ((), (), s32[]{:S(2)}) async-start(), calls=%async_computation.3 | async-start | bytes 1179648 | tf_op jit(solution)/shard_map/all_gather | solution.py:82
  158.0 0.8 copy-start.5
  175.1 9.4 copy-start.2
  184.5 7.8 copy-start.6
  193.8 124.6 %reduce-scatter.3.cloned.1.call-start = ((), (), s32[]{:S(2)}) async-start(), calls=%async_computation.4 | async-start | bytes 4456448 | tf_op jit(solution)/shard_map/reduce_scatter | solution.py:83
  238.1 0.7 copy-start.8
  238.1 80.4 %copy-start.4 = (bf16[64,1024]{1,0:T(8,128)(2,1)S(1)}, bf16[64,1024]{1,0:T(8,128)(2,1)}, u32[]{:S(2)}) copy-start(bf16[64,1024]{1,0:T(8,128)(2,1)} %param.19) | copy-start | bytes 393220
  238.1 146.9 %all-gather.5.cloned.1.call-start = ((), (), s32[]{:S(2)}) async-start(), calls=%async_computation.5 | async-start | bytes 2228224 | tf_op jit(solution)/shard_map/all_gather | solution.py:94
  340.1 636.4 %all-reduce.2.cloned.1.call-start = ((), (), s32[]{:S(2)}) async-start(), calls=%async_computation.6 | async-start | bytes 29360128 | tf_op jit(solution)/shard_map/psum | solution.py:99
  385.0 6.8 copy-start.9
  385.1 6.8 copy-start.10
  401.6 669.0 %reduce-scatter.5.cloned.1.call-start = ((), (), s32[]{:S(2)}) async-start(), calls=%async_computation.7 | async-start | bytes 4456448 | tf_op jit(solution)/shard_map/reduce_scatter | solution.py:102
  976.4 95.9 %copy-start.1 = (bf16[8,1024,128]{2,1,0:T(8,128)(2,1)S(1)}, bf16[8,1024,128]{2,1,0:T(8,128)(2,1)}, u32[]{:S(2)}) copy-start(bf16[8,1024,128]{2,1,0:T(8,128)(2,1)} %param.14) | copy-start | bytes 6291460
  988.7 81.9 %copy-start.3 = (f32[64,1024]{1,0:T(8,128)S(1)}, f32[64,1024]{1,0:T(8,128)}, u32[]{:S(2)}) copy-start(f32[64,1024]{1,0:T(8,128)} %reduce-scatter.3.cloned.1.call-done) | copy-start | bytes 786436
Sparse Core Ops, SparseCore 0:
  193.9 39.3 all-gather.2
  238.2 80.1 reduce-scatter.2
  340.2 44.8 all-gather.4
  401.7 574.6 all-reduce.1
  988.9 81.6 reduce-scatter.4
